TPU v7x, 32 devices: a whole 2x2x4 slice. The times are simulated.
32 devices in a mesh: pole: 2 (over y), row: 4 (over z), col: 4 (over x, core).
Axes of the slice: x: 2, y: 2, z: 4, core: 2. Of those that a mesh axis runs over, the one named last changes fastest.
Arguments:
- root_inverse: float32 [16384, 8192], P(('pole', 'row'), 'col'), parts along dimension 0, may hold values from -6 to 6
- lower_one: float32 [16384, 512], P(('pole', 'row'), 'col'), parts along dimension 0, may hold values from -0.0625 to 0.0625
- pattern_one: int32 [64, 4], replicated, may hold values from 0 to 1, as said below
- diag_one: float32 [256, 512], P('pole', 'col'), parts along dimension 0, may hold values from -6 to 6
- lower_two: float32 [16384, 1024], P(('pole', 'row'), 'col'), parts along dimension 0, may hold values from -0.0625 to 0.0625
- pattern_two: int32 [64, 8], replicated, may hold values from 0 to 1, as said below
- parent_two: int32 [8], replicated, may hold values from 0 to 3, as said below
- lower_parent: float32 [256, 1024], P('pole', 'col'), parts along dimension 0, may hold values from -0.5 to 0.5
- diag_two: float32 [256, 1024], P('pole', 'col'), parts along dimension 0, may hold values from -6 to 6
Outputs:
- inverse_off_one: float32 [16384, 512], P(('pole', 'row'), 'col'), parts along dimension 0
- inverse_diagonal_first: float32 [256, 512], P('pole', 'col'), parts along dimension 0
- inverse_off_two: float32 [16384, 1024], P(('pole', 'row'), 'col'), parts along dimension 0
- inverse_parent_two: float32 [256, 1024], P('pole', 'col'), parts along dimension 0
- inverse_diag_two: float32 [256, 1024], P('pole', 'col'), parts along dimension 0
There are 2 independent parts, one for each index of `pole`. A program takes and returns all parts, laid end to end along the dimension named above; an argument that names none is the same for every part. Nothing has to cross between parts.
Inputs may be any that keep to these rules, and one draw needn't show every extreme that they name: pattern_one[i, k] is 1 where root block row i lies in the structure of first-level supernode k. `parent_two`: each first-level supernode is the parent of exactly two second-level supernodes. pattern_two[i, m] is 1 only where pattern_one[i, parent_two[m]] is 1.
All inputs are finite; a program needn't handle non-finite values.
Results may differ from a plain program's by a relative error of at most 0.000088.
Values sent between devices are 32-bit elements; how exact they have to be, the bound alone decides.
No kernel may reach another device: no remote copies, remote signals or barrier semaphores. Data moves between devices by JAX's collectives and lax.ppermute only.
A program may use at most 128 MiB of HBM per device.

v0:
```python
import jax
import jax.numpy as jnp
from jax import lax
from jax.sharding import PartitionSpec as P

BLOCK_SIDE = 128


PRECISION_MODE = lax.Precision.HIGHEST


def expand_blocks(pattern, block):
    count_rows, count_cols = pattern.shape
    spread = jnp.broadcast_to(
        pattern.astype(jnp.float32)[:, None, :, None], (count_rows, block, count_cols, block)
    )
    return spread.reshape(count_rows * block, count_cols * block)


def product(left_part, right_part):
    return jnp.dot(
        left_part, right_part, precision=PRECISION_MODE, preferred_element_type=jnp.float32
    )


def guarded(left_part, right_part):
    return product(left_part, right_part)


def block_inner(masked, solved):
    rows_here = masked.shape[0]
    blocks = masked.shape[1] // BLOCK_SIDE
    inner = jnp.einsum(
        "ikb,ikc->bkc",
        masked.reshape(rows_here, blocks, BLOCK_SIDE),
        solved.reshape(rows_here, blocks, BLOCK_SIDE),
        precision=PRECISION_MODE,
    )
    return inner.reshape(BLOCK_SIDE, blocks * BLOCK_SIDE)


def column_sums(partial_sum):
    return lax.psum_scatter(partial_sum, "col", scatter_dimension=1, tiled=True)


def block_totals(stacked):
    return lax.psum(stacked, "row")


def broadcast_product(root_block, masked):
    ranks_row = lax.axis_size("row")
    ranks_col = lax.axis_size("col")
    rows_here = root_block.shape[0]
    piece_width = masked.shape[1] // ranks_row
    swapped = lax.all_to_all(
        lax.all_to_all(masked, "row", split_axis=1, concat_axis=0, tiled=True),
        "col",
        split_axis=0,
        concat_axis=1,
        tiled=True,
    )
    gathered = guarded(root_block, lax.all_gather(swapped, "row", axis=1, tiled=True))
    ordered = gathered.reshape(rows_here, ranks_row, ranks_col, piece_width).transpose(0, 2, 1, 3)
    return ordered.reshape(rows_here, ranks_row * ranks_col * piece_width)


def local(
    root_inverse,
    lower_one,
    pattern_one,
    diag_one,
    lower_two,
    pattern_two,
    parent_two,
    lower_parent,
    diag_two,
):
    rows_here = root_inverse.shape[0]
    row_blocks = rows_here // BLOCK_SIDE
    row_start = lax.axis_index("row") * row_blocks
    col_index = lax.axis_index("col")
    col_one = lower_one.shape[1] // BLOCK_SIDE
    col_two = lower_two.shape[1] // BLOCK_SIDE
    first_supernodes = pattern_one.shape[1]
    super_two = pattern_two.shape[1]
    rows_one = lax.dynamic_slice_in_dim(pattern_one, row_start, row_blocks, 0)
    rows_two = lax.dynamic_slice_in_dim(pattern_two, row_start, row_blocks, 0)
    mask_one = expand_blocks(
        lax.dynamic_slice_in_dim(rows_one, col_index * col_one, col_one, 1), BLOCK_SIDE
    )
    mask_two = expand_blocks(
        lax.dynamic_slice_in_dim(rows_two, col_index * col_two, col_two, 1), BLOCK_SIDE
    )
    masked_one = lower_one * mask_one
    masked_two = lower_two * mask_two
    owned_parent = lax.dynamic_slice_in_dim(parent_two, col_index * col_two, col_two, 0)
    select_owned_blocks = (
        owned_parent[None, :] == jnp.arange(first_supernodes, dtype=jnp.int32)[:, None]
    ).astype(jnp.float32)
    link_own = lower_parent.reshape(BLOCK_SIDE, col_two, BLOCK_SIDE)
    solved_one = column_sums(broadcast_product(root_inverse, masked_one))
    inverse_off_one = -(mask_one * solved_one)
    inverse_diagonal_first = (
        diag_one + block_totals(jnp.stack([block_inner(masked_one, solved_one)]))[0]
    )
    rows_all, link_all, diagonal_blocks_full = (
        lax.all_gather(masked_two, "col", axis=1, tiled=True),
        lax.all_gather(lower_parent, "col", axis=1, tiled=True),
        lax.all_gather(inverse_diagonal_first, "col", axis=1, tiled=True),
    )
    local_ids = col_index * col_one + jnp.arange(col_one, dtype=jnp.int32)
    pick_all = (parent_two[None, :] == local_ids[:, None]).astype(jnp.float32)
    parent_cols = jnp.einsum(
        "ikb,km->imb",
        inverse_off_one.reshape(rows_here, col_one, BLOCK_SIDE),
        pick_all,
        precision=PRECISION_MODE,
    )
    direct = broadcast_product(root_inverse, masked_two)
    direct = direct + jnp.einsum(
        "imb,bme->ime",
        parent_cols,
        link_all.reshape(BLOCK_SIDE, super_two, BLOCK_SIDE),
        precision=PRECISION_MODE,
    ).reshape(rows_here, super_two * BLOCK_SIDE)
    across_all = jnp.einsum(
        "imb,ime->bme",
        parent_cols,
        rows_all.reshape(rows_here, super_two, BLOCK_SIDE),
        precision=PRECISION_MODE,
    ).reshape(BLOCK_SIDE, super_two * BLOCK_SIDE)
    summed = column_sums(jnp.concatenate([direct, across_all], axis=0))
    solved_two = summed[:rows_here]
    across_part = summed[rows_here:]
    totals = block_totals(jnp.stack([block_inner(masked_two, solved_two), across_part]))
    parent_diagonal = jnp.einsum(
        "vfl,fo->vol",
        diagonal_blocks_full.reshape(BLOCK_SIDE, first_supernodes, BLOCK_SIDE),
        select_owned_blocks,
        precision=PRECISION_MODE,
    )
    across = totals[1].reshape(BLOCK_SIDE, col_two, BLOCK_SIDE) + jnp.einsum(
        "bmd,dme->bme", parent_diagonal, link_own, precision=PRECISION_MODE
    )
    inverse_diag_two = (
        diag_two
        + totals[0]
        + jnp.einsum("dmb,dme->bme", link_own, across, precision=PRECISION_MODE).reshape(
            BLOCK_SIDE, col_two * BLOCK_SIDE
        )
    )
    return (
        inverse_off_one,
        inverse_diagonal_first,
        -(mask_two * solved_two),
        -across.reshape(BLOCK_SIDE, col_two * BLOCK_SIDE),
        inverse_diag_two,
    )


def solution(mesh):
    return jax.shard_map(
        local,
        mesh=mesh,
        in_specs=(
            P(("pole", "row"), "col"),
            P(("pole", "row"), "col"),
            P(),
            P("pole", "col"),
            P(("pole", "row"), "col"),
            P(),
            P(),
            P("pole", "col"),
            P("pole", "col"),
        ),
        out_specs=(
            P(("pole", "row"), "col"),
            P("pole", "col"),
            P(("pole", "row"), "col"),
            P("pole", "col"),
            P("pole", "col"),
        ),
        check_vma=False,
    )
```

profile of v0, /device:TPU:0, one launch (start us, length us, event | category | flops | bytes accessed | tf_op | source)
XLA Modules:
  0.0 674.7 jit_solution(6529609036820438768)
XLA Ops:
  7.2 0.0 all-gather.4.cloned.1.call-start
  7.2 1.6 copy.31
  8.8 0.8 convert_bitcast_fusion
  9.6 0.1 broadcast_bitcast_fusion
  9.6 0.1 broadcast_multiply_fusion
  9.7 1.0 copy-done.3
  10.7 31.8 %all_to_all.64 = f32[2048,4,32]{0,2,1:T(8,128)S(1)} all-to-all(f32[2048,4,32]{0,2,1:T(8,128)S(1)} %bitcast.119), channel_id=1, replica_groups=mesh['pole'=2,'row'=4,'col'=4] {'row'}, dimensions={1} | all-to-all | bytes 2097152 | tf_op jit(solution)/shard_map/all_to_all | solution.py:56
  42.5 17.6 %all_to_all.65 = f32[4,2048,32]{1,2,0:T(8,128)} all-to-all(f32[4,2048,32]{1,2,0:T(8,128)S(1)} %bitcast.127), channel_id=1, replica_groups=mesh['pole'=2,'row'=4,'col'=4] {'col'}, dimensions={0} | all-to-all | bytes 2097152 | tf_op jit(solution)/shard_map/all_to_all | solution.py:55
  60.1 0.0 all-gather.4.cloned.1.call-update
  60.2 0.0 reduce-scatter.3.cloned.1.call-start
  60.2 79.1 %all-gather.4.cloned.1.call-done = f32[2048,512]{0,1:T(8,128)} async-done(((f32[2048,128]{0,1:T(8,128)}), f32[2048,512]{0,1:T(8,128)}) %all-gather.4.cloned.1.call-update) | async-done | bytes 4194320 | tf_op jit(solution)/shard_map/all_gather | solution.py:62
  139.3 31.7 %fusion.26 = f32[512,2048]{1,0:T(8,128)S(1)} fusion(f32[2048,512]{0,1:T(8,128)} %all-gather.4.cloned.1.call-done, f32[2048,2048]{1,0:T(8,128)} %param.9), kind=kOutput, calls=%fused_computation.41 | convolution fusion | flops 25769803776 | bytes 25165824 | tf_op jit(solution)/shard_map/dot_general | solution.py:21
  170.9 2.2 copy.32
  173.2 0.0 reduce-scatter.3.cloned.1.call-update
  173.2 0.0 all-gather.8.cloned.1.call-start
  173.2 1.9 copy.34
  175.2 0.8 dynamic-slice_convert_fusion
  175.9 0.2 broadcast_in_dim.25
  176.2 1.3 copy-done.1
  177.5 2.4 bitcast_multiply_fusion.1
  179.9 0.0 all-gather.8.cloned.1.call-update
  179.9 0.0 all-gather.6.cloned.1.call-start
  179.9 52.1 %all_to_all.66 = f32[2048,4,64]{0,2,1:T(8,128)S(1)} all-to-all(f32[2048,4,64]{0,2,1:T(8,128)} %bitcast.114), channel_id=1, replica_groups=mesh['pole'=2,'row'=4,'col'=4] {'row'}, dimensions={1} | all-to-all | bytes 4194304 | tf_op jit(solution)/shard_map/all_to_all | solution.py:56
  232.1 51.7 %all_to_all.67 = f32[4,2048,64]{1,2,0:T(8,128)} all-to-all(f32[4,2048,64]{1,2,0:T(8,128)S(1)} %bitcast.123), channel_id=1, replica_groups=mesh['pole'=2,'row'=4,'col'=4] {'col'}, dimensions={0} | all-to-all | bytes 4194304 | tf_op jit(solution)/shard_map/all_to_all | solution.py:55
  283.8 0.0 all-gather.6.cloned.1.call-update
  283.8 0.0 reduce-scatter.5.cloned.1.call-start
  283.9 10.4 %all_gather.17 = f32[128,1024]{1,0:T(8,128)S(1)} all-gather(f32[128,256]{1,0:T(8,128)S(1)} %copy-done.5), channel_id=1, replica_groups=mesh['pole'=2,'row'=4,'col'=4] {'col'}, dimensions={1}, use_global_device_ids=true | all-gather | bytes 655360 | tf_op jit(solution)/shard_map/all_gather | solution.py:108
  294.2 0.2 copy.37
  294.5 0.0 reduce-scatter.3.cloned.1.call-done
  294.5 1.3 multiply_negate_fusion
  295.8 0.3 copy.42
  296.2 10.4 %fusion.2 = f32[8,2048,128]{1,2,0:T(8,128)} fusion(f32[128,8,128]{0,2,1:T(8,128)S(1)} %bitcast.129, f32[2048,128]{1,0:T(8,128)S(1)} %copy.42, f32[8]{0:T(128)S(1)} %compare_convert_fusion), kind=kOutput, calls=%fused_computation.4 | convolution fusion | flops 3223322624 | bytes 9961504 | tf_op jit(solution)/shard_map/imb,bme->ime/dot_general | solution.py:120
  306.5 11.1 %fusion = f32[8,128,128]{2,1,0:T(8,128)S(1)} fusion(f32[2048,8,128]{0,2,1:T(8,128)} %bitcast.120, f32[2048,128]{1,0:T(8,128)S(1)} %copy.42, f32[8]{0:T(128)S(1)} %compare_convert_fusion), kind=kOutput, calls=%fused_computation.2 | convolution fusion | flops 3223322624 | bytes 9961504 | tf_op jit(solution)/shard_map/imb,ime->bme/dot_general | solution.py:126
  317.7 135.8 %all-gather.6.cloned.1.call-done = f32[2048,1024]{0,1:T(8,128)} async-done(((f32[2048,256]{0,1:T(8,128)}), f32[2048,1024]{0,1:T(8,128)}) %all-gather.6.cloned.1.call-update) | async-done | bytes 8388624 | tf_op jit(solution)/shard_map/all_gather | solution.py:62
  453.4 60.5 %fusion.27 = f32[1024,2048]{1,0:T(8,128)S(1)} fusion(f32[2048,1024]{0,1:T(8,128)} %all-gather.6.cloned.1.call-done, f32[2048,2048]{1,0:T(8,128)} %param.9), kind=kOutput, calls=%fused_computation.42 | convolution fusion | flops 51539607552 | bytes 33554432 | tf_op jit(solution)/shard_map/dot_general | solution.py:21
  513.9 3.9 copy.35
  517.8 11.8 %bitcast_add_fusion = f32[2048,1024]{0,1:T(8,128)} fusion(f32[8,2048,128]{1,2,0:T(8,128)} %fusion.2, f32[2048,4,4,64]{0,3,1,2:T(8,128)} %copy.35), kind=kLoop, calls=%fused_computation.1 | loop fusion | flops 2097152 | bytes 25165824 | tf_op jit(solution)/shard_map/add | solution.py:120
  529.5 7.6 %pad_maximum_fusion = f32[2176,1024]{0,1:T(8,128)} fusion(f32[128,1024]{0,1:T(8,128)S(1)} %bitcast.128, f32[2048,1024]{0,1:T(8,128)} %bitcast_add_fusion), kind=kLoop, calls=%fused_computation | loop fusion | flops 2228224 | bytes 17825792 | tf_op jit(solution)/shard_map/concatenate | solution.py:132
  537.1 0.0 reduce-scatter.5.cloned.1.call-update
  537.1 0.0 all-reduce.3.cloned.1.call-start
  537.2 1.1 copy-done.4
  538.3 2.9 convolution_bitcast_fusion.1
  541.2 69.4 %reduce-scatter.5.cloned.1.call-done = f32[2176,256]{0,1:T(8,128)} async-done(((f32[2176,1024]{0,1:T(8,128)}), f32[2176,256]{0,1:T(8,128)}) %reduce-scatter.5.cloned.1.call-update) | async-done | bytes 2228240 | tf_op jit(solution)/shard_map/reduce_scatter | solution.py:43
  610.5 4.7 fusion.10
  615.2 2.0 fusion.28
  617.3 0.9 slice_bitcast_fusion.1
  618.2 0.7 pad_maximum_fusion.1
  618.9 0.0 all-reduce.3.cloned.1.call-update
  619.0 0.1 dynamic_slice.13
  619.0 0.1 copy.33
  619.1 0.1 copy.40
  619.2 2.9 copy.44
  622.1 33.3 %all-reduce.3.cloned.1.call-done = (f32[128,128]{0,1:T(8,128)}, f32[2,128,256]{1,2,0:T(8,128)}) async-done(((f32[128,128]{0,1:T(8,128)}, f32[2,128,256]{1,2,0:T(8,128)}), (f32[128,128]{0,1:T(8,128)}, f32[2,128,256]{1,2,0:T(8,128)})) %all-reduce.3.cloned.1.call-update) | async-done | bytes 327696 | tf_op jit(solution)/shard_map/psum | solution.py:47
  655.5 0.8 add.40
  656.3 0.7 copy.43
  657.0 5.8 all_gather.19
  662.8 0.9 slice.18
  663.7 0.1 copy.48
  663.9 0.4 fusion.22
  664.3 0.4 fusion.25
  664.7 0.8 copy.45
  665.5 0.3 fusion.13
  665.7 0.9 fusion.16
  666.7 0.8 copy.46
  (17 shorter events, 0.0 us)
Async XLA Ops:
  7.2 132.1 %all-gather.4.cloned.1.call-start = ((), (), s32[]{:S(2)}) async-start(), calls=%async_computation.6 | async-start | bytes 5242880 | tf_op jit(solution)/shard_map/all_gather | solution.py:62
  9.7 1.0 copy-start.3
  60.2 234.3 %reduce-scatter.3.cloned.1.call-start = ((), (), s32[]{:S(2)}) async-start(), calls=%async_computation.7 | async-start | bytes 5242880 | tf_op jit(solution)/shard_map/reduce_scatter | solution.py:43
  173.2 133.4 %all-gather.8.cloned.1.call-start = ((), (), s32[]{:S(2)}) async-start(), calls=%async_computation.9 | async-start | bytes 10485760 | tf_op jit(solution)/shard_map/all_gather | solution.py:107
  176.2 1.3 copy-start.1
  177.5 106.4 %copy-start.5 = (f32[128,256]{1,0:T(8,128)S(1)}, f32[128,256]{1,0:T(8,128)}, u32[]{:S(2)}) copy-start(f32[128,256]{1,0:T(8,128)} %param.16) | copy-start | bytes 393220
  179.9 114.6 %copy-start.8 = (s32[8]{0:T(128)S(1)}, s32[8]{0:T(128)}, u32[]{:S(2)}) copy-start(s32[8]{0:T(128)} %param.15) | copy-start | bytes 100
  179.9 273.5 %all-gather.6.cloned.1.call-start = ((), (), s32[]{:S(2)}) async-start(), calls=%async_computation.8 | async-start | bytes 10485760 | tf_op jit(solution)/shard_map/all_gather | solution.py:62
  283.8 326.7 %reduce-scatter.5.cloned.1.call-start = ((), (), s32[]{:S(2)}) async-start(), calls=%async_computation.10 | async-start | bytes 11141120 | tf_op jit(solution)/shard_map/reduce_scatter | solution.py:43
  296.2 21.5 %copy-start.2 = (f32[2048,128]{1,0:T(8,128)}, f32[2048,128]{1,0:T(8,128)S(1)}, u32[]{:S(2)}) copy-start(f32[2048,128]{1,0:T(8,128)S(1)} %copy.42) | copy-start | bytes 3145732
  537.1 1.2 copy-start.4
  537.1 78.2 %copy-start = (f32[2048,256]{0,1:T(8,128)S(1)}, f32[2048,256]{0,1:T(8,128)}, u32[]{:S(2)}) copy-start(f32[2048,256]{0,1:T(8,128)} %bitcast_multiply_fusion.1) | copy-start | bytes 6291460
  537.1 81.9 %copy-start.7 = (f32[128,128]{1,0:T(8,128)S(1)}, f32[128,128]{1,0:T(8,128)}, u32[]{:S(2)}) copy-start(f32[128,128]{1,0:T(8,128)} %param.12) | copy-start | bytes 196612
  537.1 82.0 %copy-start.6 = (f32[128,256]{1,0:T(8,128)S(1)}, f32[128,256]{1,0:T(8,128)}, u32[]{:S(2)}) copy-start(f32[128,256]{1,0:T(8,128)} %param.17) | copy-start | bytes 393220
  537.1 118.3 %all-reduce.3.cloned.1.call-start = ((), (), s32[]{:S(2)}) async-start(), calls=%async_computation.11 | async-start | bytes 655360 | tf_op jit(solution)/shard_map/psum | solution.py:47
Sparse Core Ops, SparseCore 0:
  60.3 78.9 all-gather.3
  173.3 43.0 reduce-scatter.2
  218.6 83.5 all-gather.7
  303.7 149.6 all-gather.5
  537.2 73.2 reduce-scatter.4
  619.1 36.3 all-reduce.2
where the time goes:
time: 683 us; the launch traced here: 675 us
  waiting for transfers between devices  318 us (47%)
  blocking collectives  169 us (25%)
  matrix products  120 us (18%)
  other arithmetic  31.8 us (5%)
  local copies, waits for them, and re-layouts  21.2 us (3%)
  between operations  14.8 us (2%)
    all_gather x2, waiting for transfers between devices, broadcast_product(): lax.all_gather(swapped, 'row', axis=1, tiled=True)  215 us
    dot_general x2, matrix products, product(): jnp.dot(left_part, right_part, precision=PRECISION_MODE, preferred_elemen...  92.1 us
    all_to_all x2, blocking collectives, broadcast_product(): lax.all_to_all(masked, 'row', split_axis=1, concat_axis=0, tiled=True)  83.9 us
    reduce_scatter x2, waiting for transfers between devices, column_sums(): return lax.psum_scatter(partial_sum, 'col', scatter_dimension=1, tiled=True)  69.4 us
    all_to_all x2, blocking collectives, broadcast_product(): lax.all_to_all(lax.all_to_all(masked, 'row', split_axis=1, concat_axis=0,...  69.3 us
    psum x1, waiting for transfers between devices, block_totals(): return lax.psum(stacked, 'row')  33.3 us
  transfers between devices with their start and end apart: 6, of which 4 were waited for; matrix products, arithmetic and copies ran while one was open for 5% of the time, Pallas kernels for 0%

commit v1 on v0

v1 whole, which is shorter than its diff:
```python
import functools

import jax
import jax.numpy as jnp
from jax import lax
from jax.experimental import pallas as pl
from jax.experimental.pallas import tpu as pltpu
from jax.sharding import PartitionSpec as P

SIDE = 128
PAIR = 2 * SIDE
GROUP_ROWS = 2
GROUP_COLS = 4
EXACT = lax.Precision.HIGHEST
VMEM_BYTES = 56 * 1024 * 1024
ROOT_COPIES = 8

SMEM_SPEC = pl.BlockSpec(memory_space=pltpu.SMEM)
VMEM_SPEC = pl.BlockSpec(memory_space=pltpu.VMEM)
ANY_SPEC = pl.BlockSpec(memory_space=pl.ANY)


def shape_f32(rows, cols):
    return jax.ShapeDtypeStruct((rows, cols), jnp.float32)


def call(body, outs, smem, vmem, scratch=(), far=()):
    return pl.pallas_call(
        body,
        out_shape=outs,
        in_specs=[SMEM_SPEC] * len(smem) + [ANY_SPEC] * len(far) + [VMEM_SPEC] * len(vmem),
        out_specs=jax.tree.map(lambda _: VMEM_SPEC, outs),
        scratch_shapes=list(scratch),
        compiler_params=pltpu.CompilerParams(vmem_limit_bytes=VMEM_BYTES),
    )(*smem, *far, *vmem)


def halves(value):
    high = value.astype(jnp.bfloat16)
    low = (value - high.astype(jnp.float32)).astype(jnp.bfloat16)
    return high, low


def beside(value):
    return jnp.concatenate(halves(value), axis=1)


def above(value):
    return jnp.concatenate(halves(value), axis=0)


def fold_cols(value):
    return value[:, :SIDE] + value[:, SIDE:]


def fold_all(value):
    rows = value.shape[0] // 2
    return fold_cols(value[:rows] + value[rows:])


def inner(left, right):
    return fold_all(
        lax.dot_general(
            beside(left),
            beside(right),
            (((0,), (0,)), ((), ())),
            preferred_element_type=jnp.float32,
        )
    )


def block_at(index):
    return pl.ds(pl.multiple_of(index * SIDE, SIDE), SIDE)


def rounded(count, step):
    return -(-count // step) * step


def pack_body(row_blocks, where_ref, pattern, source, target):
    row_start = where_ref[0] * row_blocks
    col_index = where_ref[1]
    filled = jnp.int32(0)
    owned = source.shape[1] // SIDE
    for local in range(owned):

        def step(block, count, local=local):
            active = pattern[row_start + block, col_index * owned + local] > 0

            @pl.when(active)
            def _():
                target[block_at(count), :] = source[block_at(block), local * SIDE : (local + 1) * SIDE]

            return count + active.astype(jnp.int32)

        filled = lax.fori_loop(0, row_blocks, step, filled)


def pack(where, pattern, source, capacity):
    return call(
        functools.partial(pack_body, source.shape[0] // SIDE),
        shape_f32(capacity * SIDE, SIDE),
        [where, pattern],
        [source],
    )


def split_body(source, target):
    cols = source.shape[1]
    high, low = halves(source[...])
    target[:, :cols] = high
    target[:, cols:] = low


def split_root(root):
    rows, cols = root.shape
    step = min(rows, 256)
    return pl.pallas_call(
        split_body,
        out_shape=jax.ShapeDtypeStruct((rows, 2 * cols), jnp.bfloat16),
        grid=(rows // step,),
        in_specs=[pl.BlockSpec((step, cols), lambda i: (i, 0))],
        out_specs=pl.BlockSpec((step, 2 * cols), lambda i: (i, 0)),
        compiler_params=pltpu.CompilerParams(vmem_limit_bytes=VMEM_BYTES),
    )(root)


def line_body(ranks_col, piece_rows, where_ref, bases, *refs):
    parts, rest = refs[:ranks_col], refs[ranks_col:]
    outs, line = rest[:ranks_col], rest[ranks_col]
    col_index = where_ref[1]
    for hop in range(ranks_col):
        owner = col_index ^ hop
        base = bases[owner]

        def step(slot, carry, hop=hop, base=base):
            line[block_at(base + slot), :] = parts[hop][block_at(slot), :]
            return carry

        lax.fori_loop(0, bases[owner + 1] - base, step, jnp.int32(0))
    for step in range(ranks_col):
        at = ((col_index ^ step) * ranks_col + step) * piece_rows
        outs[step][...] = line[pl.ds(pl.multiple_of(at, 8), piece_rows), :]


class Plan:
    def __init__(self, rows, cols):
        self.rows = rounded(rows, GROUP_COLS)
        self.cols = rounded(cols, GROUP_COLS)
        self.row_block = 2
        self.row_slot = self.row_block + self.rows
        self.row_first = self.row_slot + self.rows
        self.col_block = self.row_first + self.rows
        self.col_slot = self.col_block + self.cols
        self.stride = self.col_slot + self.cols


def listed(active, values, length):
    blocks = active.shape[0]
    before = (jnp.arange(blocks)[None, :] < jnp.arange(blocks)[:, None]).astype(jnp.int32)
    rank = jnp.sum(before[:, :, None] * active[None], axis=1)
    count = jnp.sum(active, axis=0)
    wanted = jnp.minimum(jnp.arange(length)[:, None], count[None, :] - 1)
    hit = jnp.where(rank[None] == wanted[:, None, :], active[None], 0)
    return [jnp.sum(hit * value[None], axis=1).T for value in values], count


def make_plan(active_row, slot_row, first_row, active_col, slot_col):
    plan = Plan(active_row.shape[0], active_col.shape[0])
    number = lambda active: jnp.broadcast_to(jnp.arange(active.shape[0])[:, None], active.shape)
    rows, count_rows = listed(active_row, [number(active_row), slot_row, first_row], plan.rows)
    cols, count_cols = listed(active_col, [number(active_col), slot_col], plan.cols)
    table = jnp.concatenate([count_rows[:, None], count_cols[:, None], *rows, *cols], axis=1)
    return plan, table.astype(jnp.int32).reshape(-1)


def root_body(plan, ranks_col, owned, capacity, second, where_ref, table, root_ref, gathered, *refs):
    if second:
        known, *refs = refs
        outs, refs = refs[:ranks_col], refs[ranks_col:]
    else:
        outs, everything, *refs = refs[:ranks_col], *refs[ranks_col:]
    weights, root, starts, arrived = refs
    col_index = where_ref[1]
    nodes = ranks_col * owned
    cols = root.shape[1] // 2
    share = root.shape[0] // arrived.shape[0]
    copies = [
        pltpu.make_async_copy(
            root_ref.at[pl.ds(t * share, share), :], root.at[pl.ds(t * share, share), :], arrived.at[t]
        )
        for t in range(arrived.shape[0])
    ]
    for copy in copies:
        copy.start()

    def prepare(node, base):
        starts[node] = base
        at = node * plan.stride
        count = table[at + 1]

        def fill(t, carry):
            slot = table[at + plan.col_slot + t]
            weights[block_at(base + t), :] = beside(gathered[block_at(slot), :])
            return carry

        def clear(t, carry):
            weights[block_at(base + t), :] = jnp.zeros((SIDE, PAIR), jnp.bfloat16)
            return carry

        lax.fori_loop(0, count, fill, jnp.int32(0))
        upper = (count + GROUP_COLS - 1) // GROUP_COLS * GROUP_COLS
        lax.fori_loop(count, upper, clear, jnp.int32(0))
        return base + upper

    lax.fori_loop(0, nodes, prepare, jnp.int32(0))
    for copy in copies:
        copy.wait()

    def per_node(node, carry):
        at = node * plan.stride
        base = starts[node]
        hop = (node // owned) ^ col_index
        groups = (table[at + 1] + GROUP_COLS - 1) // GROUP_COLS

        def row_group(group, carry):
            blocks = [table[at + plan.row_block + group * GROUP_ROWS + t] for t in range(GROUP_ROWS)]

            def col_group(step, total):
                columns = [
                    pl.multiple_of(table[at + plan.col_block + step * GROUP_COLS + q] * SIDE, SIDE)
                    for q in range(GROUP_COLS)
                ]
                tiles = [
                    jnp.concatenate(
                        [root[block_at(block), pl.ds(shift + column, SIDE)] for column in columns], axis=1
                    )
                    for shift in (0, cols)
                    for block in blocks
                ]
                start = pl.multiple_of((base + step * GROUP_COLS) * SIDE, GROUP_COLS * SIDE)
                made = jnp.dot(
                    jnp.concatenate(tiles, axis=0),
                    weights[pl.ds(start, GROUP_COLS * SIDE), :],
                    preferred_element_type=jnp.float32,
                )
                return total + fold_all(made)

            total = lax.fori_loop(
                0, groups, col_group, jnp.zeros((GROUP_ROWS * SIDE, SIDE), jnp.float32)
            )
            for t in range(GROUP_ROWS):
                slot = table[at + plan.row_slot + group * GROUP_ROWS + t]
                value = total[t * SIDE : (t + 1) * SIDE]
                if second:
                    value = value - known[block_at(slot), :]
                else:
                    everything[block_at(slot), :] = value
                for other in range(ranks_col):

                    @pl.when(hop == other)
                    def _(other=other, slot=slot, value=value):
                        outs[other][block_at(slot - other * capacity), :] = value

            return carry

        return lax.fori_loop(0, (table[at] + GROUP_ROWS - 1) // GROUP_ROWS, row_group, carry)

    lax.fori_loop(0, nodes, per_node, jnp.int32(0))


def root_partials(where, plan, table, root, gathered, ranks_col, owned, capacity, known=None):
    rows, wide = root.shape
    nodes = ranks_col * owned
    room = min(nodes * plan.cols, rounded(gathered.shape[0] // SIDE, GROUP_COLS) + nodes * GROUP_COLS)
    copies = ROOT_COPIES if rows % (ROOT_COPIES * 16) == 0 else 1
    outs = [shape_f32(capacity * SIDE, SIDE)] * ranks_col
    if known is None:
        outs = outs + [shape_f32(ranks_col * capacity * SIDE, SIDE)]
    return call(
        functools.partial(root_body, plan, ranks_col, owned, capacity, known is not None),
        outs,
        [where, table],
        [gathered] if known is None else [gathered, known],
        [
            pltpu.VMEM((room * SIDE, PAIR), jnp.bfloat16),
            pltpu.VMEM((rows, wide), jnp.bfloat16),
            pltpu.SMEM((nodes,), jnp.int32),
            pltpu.SemaphoreType.DMA((copies,)),
        ],
        [root],
    )


def link_body(plan, table, firsts, link, out):
    nodes = link.shape[1] // SIDE

    def per_node(node, carry):
        at = node * plan.stride
        block = beside(link[:, block_at(node)])

        def step(t, carry):
            first = table[at + plan.row_first + t]
            slot = table[at + plan.row_slot + t]
            made = jnp.dot(above(firsts[block_at(first), :]), block, preferred_element_type=jnp.float32)
            out[block_at(slot), :] = fold_all(made)
            return carry

        return lax.fori_loop(0, table[at], step, carry)

    lax.fori_loop(0, nodes, per_node, jnp.int32(0))


def first_body(row_blocks, ranks_col, where_ref, pattern, position, pattern_two, position_two, kids, *refs):
    mine, near, far, packed, *rest = refs
    blocks_two, (off, sums, total) = rest[:ranks_col], rest[ranks_col:]
    row_start = where_ref[0] * row_blocks
    col_index = where_ref[1]
    owned = off.shape[1] // SIDE
    owned_two = pattern_two.shape[1] // ranks_col
    total[...] = mine[...] + near[...] + far[...]
    sums[...] = jnp.zeros(sums.shape, jnp.float32)
    for local in range(owned):
        node = col_index * owned + local
        lanes = slice(local * SIDE, (local + 1) * SIDE)

        def step(block, carry):
            place = row_start + block
            slot = position[place, node]
            active = pattern[place, node] > 0

            @pl.when(active)
            def _():
                value = total[block_at(slot), :]
                off[block_at(block), lanes] = -value
                sums[0:SIDE, lanes] += inner(packed[block_at(slot), :], value)

            @pl.when(jnp.logical_not(active))
            def _():
                off[block_at(block), lanes] = jnp.zeros((SIDE, SIDE), jnp.float32)

            for kid in range(2):
                child = kids[2 * local + kid]
                hop = col_index ^ (child // owned_two)
                slot_two = position_two[place, child]

                @pl.when(pattern_two[place, child] > 0)
                def _(kid=kid, hop=hop, slot_two=slot_two):
                    for other in range(ranks_col):

                        @pl.when(hop == other)
                        def _(other=other):
                            sums[(1 + kid) * SIDE : (2 + kid) * SIDE, lanes] += inner(
                                total[block_at(slot), :], blocks_two[other][block_at(slot_two), :]
                            )

            return carry

        lax.fori_loop(0, row_blocks, step, jnp.int32(0))


def second_body(row_blocks, where_ref, pattern, position, mine, near, far, packed, off, sums, total):
    row_start = where_ref[0] * row_blocks
    col_index = where_ref[1]
    owned = off.shape[1] // SIDE
    total[...] = mine[...] + near[...] + far[...]
    sums[...] = jnp.zeros(sums.shape, jnp.float32)
    for local in range(owned):
        node = col_index * owned + local
        lanes = slice(local * SIDE, (local + 1) * SIDE)

        def step(block, carry):
            place = row_start + block
            slot = position[place, node]
            active = pattern[place, node] > 0

            @pl.when(active)
            def _():
                value = total[block_at(slot), :]
                off[block_at(block), lanes] = -value
                sums[:, lanes] += inner(packed[block_at(slot), :], value)

            @pl.when(jnp.logical_not(active))
            def _():
                off[block_at(block), lanes] = jnp.zeros((SIDE, SIDE), jnp.float32)

            return carry

        lax.fori_loop(0, row_blocks, step, jnp.int32(0))


def tail_body(kids, diag, sums, link, diagonal, made):
    owned = diag.shape[1] // SIDE
    for local in range(owned):
        lanes = slice(local * SIDE, (local + 1) * SIDE)
        own = diag[:, lanes] + sums[0:SIDE, lanes]
        diagonal[:, lanes] = own
        for kid in range(2):
            step = link[:, block_at(kids[2 * local + kid])]
            share = sums[(1 + kid) * SIDE : (2 + kid) * SIDE, lanes]
            across = jnp.dot(own, step, precision=EXACT, preferred_element_type=jnp.float32) - share
            at = (2 * local + kid) * SIDE
            made[at : at + SIDE, 0:SIDE] = -across
            made[at : at + SIDE, SIDE:PAIR] = inner(step, across)


def swap_col(value, hop):
    ranks = lax.axis_size("col")
    return lax.ppermute(value, "col", [(c, c ^ hop) for c in range(ranks)])


def gather_col(value):
    across = swap_col(value, 2)
    return [value, swap_col(value, 1), across, swap_col(across, 1)]


def exchange_col(value, col_index, chunk):
    piece = lambda hop: lax.dynamic_slice_in_dim(value, (col_index ^ hop) * chunk, chunk, 0)
    moved = [swap_col(piece(hop), hop) for hop in (3, 2, 1)]
    return jnp.concatenate([piece(0), moved[2], moved[1], moved[0]], axis=0)


def turn(pieces):
    ranks = len(pieces)
    return jnp.concatenate(
        [
            lax.ppermute(
                piece,
                ("row", "col"),
                [(r * ranks + c, (c ^ u) * ranks + r) for r in range(ranks) for c in range(ranks)],
            )
            for u, piece in enumerate(pieces)
        ],
        axis=0,
    )


def scatter_col(parts):
    relay = parts[2] + swap_col(parts[3], 1)
    return parts[0], swap_col(parts[1], 1), swap_col(relay, 2), relay


def sum_row(value):
    ranks = lax.axis_size("row")
    reach = 1
    while reach < ranks:
        value = value + lax.ppermute(value, "row", [(r, r ^ reach) for r in range(ranks)])
        reach *= 2
    return value


def counts(pattern, row_blocks, ranks_col):
    blocks, nodes = pattern.shape
    return jnp.sum(
        pattern.reshape(blocks // row_blocks, row_blocks, ranks_col, nodes // ranks_col), axis=(1, 3)
    )


def positions(pattern, row_blocks, ranks_col):
    blocks, nodes = pattern.shape
    owned = nodes // ranks_col
    many = owned * row_blocks
    flat = (
        pattern.reshape(blocks // row_blocks, row_blocks, ranks_col, owned)
        .transpose(0, 2, 3, 1)
        .reshape(blocks // row_blocks, ranks_col, many)
    )
    before = (jnp.arange(many)[None, :] < jnp.arange(many)[:, None]).astype(jnp.int32)
    rank = jnp.sum(flat[:, :, None, :] * before[None, None], axis=-1)
    return (
        rank.reshape(blocks // row_blocks, ranks_col, owned, row_blocks)
        .transpose(0, 3, 1, 2)
        .reshape(blocks, nodes)
        .astype(jnp.int32)
    )


def after(value, *others):
    return lax.optimization_barrier((value, *others))[0]


def sparse_plan(
    capacities,
    root_inverse,
    lower_one,
    pattern_one,
    diag_one,
    lower_two,
    pattern_two,
    parent_two,
    lower_parent,
    diag_two,
):
    capacity_one, capacity_two, capacity_line = capacities
    rows_here, cols_here = root_inverse.shape
    row_blocks = rows_here // SIDE
    col_blocks = cols_here // SIDE
    ranks_row = lax.axis_size("row")
    ranks_col = lax.axis_size("col")
    turned = ranks_row == ranks_col
    group = ranks_row // ranks_col
    row_index = lax.axis_index("row")
    col_index = lax.axis_index("col")
    owned_one = lower_one.shape[1] // SIDE
    owned_two = lower_two.shape[1] // SIDE
    where = jnp.stack([row_index, col_index]).astype(jnp.int32)

    packed_one = pack(where, pattern_one, lower_one, capacity_one)
    rows_one = lax.all_gather(packed_one, "row", axis=0, tiled=True)
    packed_two = pack(where, pattern_two, after(lower_two, packed_one), capacity_two)
    beside_two = gather_col(packed_two)

    position_one = positions(pattern_one, row_blocks, ranks_col)
    position_two = positions(pattern_two, row_blocks, ranks_col)
    held_two = counts(pattern_two, row_blocks, ranks_col)
    base_two = jnp.concatenate([jnp.zeros((ranks_row, 1), jnp.int32), jnp.cumsum(held_two, axis=1)], axis=1)
    base_two = base_two.astype(jnp.int32)
    own_rows = lambda value: lax.dynamic_slice_in_dim(value, row_index * row_blocks, row_blocks, 0)
    own_cols = lambda value: lax.dynamic_slice_in_dim(value, col_index * col_blocks, col_blocks, 0)
    hop_one = ((jnp.arange(pattern_one.shape[1]) // owned_one) ^ col_index)[None, :]
    hop_two = ((jnp.arange(pattern_two.shape[1]) // owned_two) ^ col_index)[None, :]
    part = (jnp.arange(col_blocks) // row_blocks)[:, None]
    give_one = hop_one * capacity_one + own_rows(position_one)
    give_two = hop_two * capacity_two + own_rows(position_two)
    take_one = (hop_one * group + part) * capacity_one + own_cols(position_one)
    if turned:
        start_two = lax.dynamic_slice_in_dim(base_two, col_index, 1, 0)[:, :ranks_col]
        take_two = jnp.repeat(start_two, owned_two, axis=1) + own_cols(position_two)
    else:
        take_two = (hop_two * group + part) * capacity_two + own_cols(position_two)
    elder = (parent_two[None, :] == jnp.arange(pattern_one.shape[1])[:, None]).astype(jnp.int32)
    first_two = jnp.sum(give_one[:, :, None] * elder[None], axis=1)
    plan, table_one = make_plan(
        own_rows(pattern_one), give_one, give_one, own_cols(pattern_one), take_one
    )
    _, table_two = make_plan(own_rows(pattern_two), give_two, first_two, own_cols(pattern_two), take_two)

    link = jnp.stack(gather_col(lower_parent)).reshape(ranks_col, SIDE, owned_two * SIDE)
    link = jnp.concatenate(
        [
            lax.dynamic_index_in_dim(link, col_index ^ owner, 0, keepdims=False)
            for owner in range(ranks_col)
        ],
        axis=1,
    )
    local_ids = col_index * owned_one + jnp.arange(owned_one, dtype=jnp.int32)
    is_kid = parent_two[None, :] == local_ids[:, None]
    ids = jnp.arange(parent_two.shape[0], dtype=jnp.int32)[None, :]
    first_kid = jnp.min(jnp.where(is_kid, ids, ids.shape[1] - 1), axis=1)
    last_kid = jnp.max(jnp.where(is_kid, ids, 0), axis=1)
    kids = jnp.stack([first_kid, last_kid], axis=1).reshape(2 * owned_one)
    root = split_root(root_inverse)
    if turned:
        piece_rows = capacity_line * SIDE // (ranks_col * ranks_col)
        own_base = lax.dynamic_slice_in_dim(base_two, row_index, 1, 0)[0]
        pieces = call(
            functools.partial(line_body, ranks_col, piece_rows),
            [shape_f32(piece_rows, SIDE)] * ranks_col,
            [where, own_base],
            [*beside_two[:3], after(beside_two[3], root, table_one, table_two, link, kids)],
            [pltpu.VMEM((capacity_line * SIDE, SIDE), jnp.float32)],
        )
        ahead_two = turn(pieces)
    else:
        ahead_two = packed_two
    rows_two = lax.all_gather(ahead_two, "row", axis=0, tiled=True)
    rows_one = after(rows_one, root, ahead_two, link, table_one, table_two, kids)
    gathered_one = exchange_col(rows_one, col_index, group * capacity_one * SIDE)
    *partial_one, every_one = root_partials(
        where, plan, table_one, root, gathered_one, ranks_col, owned_one, capacity_one
    )
    mine_one, near_one, far_one, relay_one = scatter_col(partial_one)
    every_one = after(every_one, relay_one)
    known_two = call(
        functools.partial(link_body, plan),
        shape_f32(ranks_col * capacity_two * SIDE, SIDE),
        [table_two],
        [every_one, link],
    )
    far_one = after(far_one, known_two)
    off_one, inner_one, _ = call(
        functools.partial(first_body, row_blocks, ranks_col),
        [
            shape_f32(rows_here, owned_one * SIDE),
            shape_f32(3 * SIDE, owned_one * SIDE),
            shape_f32(capacity_one * SIDE, SIDE),
        ],
        [where, pattern_one, position_one, pattern_two, position_two, kids],
        [mine_one, near_one, far_one, packed_one, *beside_two],
    )
    rows_two = after(rows_two, known_two, off_one)
    if turned:
        gathered_two = rows_two
    else:
        gathered_two = exchange_col(rows_two, col_index, group * capacity_two * SIDE)
    partial_two = root_partials(
        where, plan, table_two, root, gathered_two, ranks_col, owned_two, capacity_two, known_two
    )
    *sums_two, relay_two = scatter_col(partial_two)

    inner_one = after(inner_one, relay_two)
    inner_one = sum_row(inner_one)
    diagonal_first, made = call(
        tail_body,
        [shape_f32(SIDE, owned_one * SIDE), shape_f32(2 * owned_one * SIDE, PAIR)],
        [kids],
        [diag_one, inner_one, link],
    )
    made_all = jnp.concatenate(gather_col(made), axis=0).reshape(ranks_col, owned_one, 2, SIDE, PAIR)
    chosen = []
    for local in range(owned_two):
        child = col_index * owned_two + local
        parent = lax.dynamic_index_in_dim(parent_two, child, 0, keepdims=False)
        later = jnp.sum(jnp.logical_and(parent_two == parent, ids[0] < child).astype(jnp.int32))
        hop = col_index ^ (parent // owned_one)
        chosen.append(
            lax.dynamic_slice(
                made_all, (hop, parent % owned_one, later, 0, 0), (1, 1, 1, SIDE, PAIR)
            ).reshape(SIDE, PAIR)
        )
    minus_across = jnp.concatenate([c[:, :SIDE] for c in chosen], axis=1)
    known = diag_two + jnp.concatenate([c[:, SIDE:] for c in chosen], axis=1)

    off_two, inner_two, _ = call(
        functools.partial(second_body, row_blocks),
        [
            shape_f32(rows_here, owned_two * SIDE),
            shape_f32(SIDE, owned_two * SIDE),
            shape_f32(capacity_two * SIDE, SIDE),
        ],
        [where, pattern_two, position_two],
        [*sums_two, packed_two],
    )
    return off_one, diagonal_first, off_two, minus_across, known + sum_row(inner_two)


def ladder(full_one, full_two, ranks_col):
    steps = []
    for one, two, line in ((10, 15, 52), (12, 18, 62), (16, 32, 128)):
        step = (
            rounded(one * full_one, 16) // 16,
            rounded(two * full_two, 32) // 32,
            rounded(line * full_two * ranks_col, 128) // 128,
        )
        if step not in steps:
            steps.append(step)
    return steps


def level_body(steps, row_blocks, ranks_col, one, two, level):
    def held(pattern):
        blocks, nodes = pattern.shape
        ranks_row = blocks // row_blocks
        rows = lax.broadcasted_iota(jnp.int32, (ranks_row, blocks), 0)
        inside = lax.broadcasted_iota(jnp.int32, (ranks_row, blocks), 1) // row_blocks == rows
        cols = lax.broadcasted_iota(jnp.int32, (nodes, ranks_col), 1)
        owner = lax.broadcasted_iota(jnp.int32, (nodes, ranks_col), 0) // (nodes // ranks_col) == cols
        by_row = jnp.dot(
            inside.astype(jnp.float32), pattern[...].astype(jnp.float32), preferred_element_type=jnp.float32
        )
        return jnp.dot(by_row, owner.astype(jnp.float32), preferred_element_type=jnp.float32)

    held_one, held_two = held(one), held(two)
    most = (jnp.max(held_one), jnp.max(held_two), jnp.max(jnp.sum(held_two, axis=1, keepdims=True)))
    found = jnp.int32(0)
    for step in steps[:-1]:
        over = functools.reduce(jnp.logical_or, [m > limit for m, limit in zip(most, step)])
        found = found + over.astype(jnp.int32)
    level[0] = found


def local(root_inverse, lower_one, pattern_one, diag_one, lower_two, pattern_two, *others):
    row_blocks = root_inverse.shape[0] // SIDE
    ranks_col = lax.axis_size("col")
    steps = ladder(
        row_blocks * lower_one.shape[1] // SIDE, row_blocks * lower_two.shape[1] // SIDE, ranks_col
    )
    operands = (root_inverse, lower_one, pattern_one, diag_one, lower_two, pattern_two, *others)
    if len(steps) == 1:
        return sparse_plan(steps[0], *operands)
    level = pl.pallas_call(
        functools.partial(level_body, steps, row_blocks, ranks_col),
        out_shape=jax.ShapeDtypeStruct((1,), jnp.int32),
        in_specs=[VMEM_SPEC, VMEM_SPEC],
        out_specs=SMEM_SPEC,
    )(pattern_one, pattern_two)
    return lax.switch(level[0], [functools.partial(sparse_plan, step) for step in steps], *operands)


def solution(mesh):
    return jax.shard_map(
        local,
        mesh=mesh,
        in_specs=(
            P(("pole", "row"), "col"),
            P(("pole", "row"), "col"),
            P(),
            P("pole", "col"),
            P(("pole", "row"), "col"),
            P(),
            P(),
            P("pole", "col"),
            P("pole", "col"),
        ),
        out_specs=(
            P(("pole", "row"), "col"),
            P("pole", "col"),
            P(("pole", "row"), "col"),
            P("pole", "col"),
            P("pole", "col"),
        ),
        check_vma=False,
    )
```

time: 683 us -> 335 us (0.49); the launches traced: 675 us -> 336 us
  waiting for transfers between devices: 318 us -> 104 us
  blocking collectives: 169 us -> 0 us
  matrix products: 120 us -> 0 us
  Pallas kernels: 0 us -> 101 us
  starting transfers between devices: 0.25 us -> 50.5 us
  local copies, waits for them, and re-layouts: 21.2 us -> 30.1 us
    all_gather x3 -> x2, waiting for transfers between devices: 215 us -> 0.02 us  [the longest x1 0.02 us: sparse_plan(): rows_one = lax.all_gather(packed_one, 'row', axis=0, tiled=True)]
    all_to_all x4 -> x0, blocking collectives: 153 us -> none  [the longest x2 83.9 us: broadcast_product(): lax.all_to_all(masked, 'row', split_axis=1, concat_axis=0, tiled=True)]
    dot_general x9 -> x0, matrix products: 120 us -> none  [the longest x2 92.1 us: product(): jnp.dot(left_part, right_part, precision=PRECISION_MODE, preferred_elemen...]
    ppermute x0 -> x26, waiting for transfers between devices: none -> 104 us  [the longest x18 67.3 us: swap_col(): return lax.ppermute(value, 'col', [(c, c ^ hop) for c in range(ranks)])]
    pallas_call x0 -> x11, Pallas kernels: none -> 101 us  [the longest x9 84.8 us: call(): pl.pallas_call(body, out_shape=outs, in_specs=[SMEM_SPEC] * len(smem) + [...]
    reduce_scatter x2 -> x0, waiting for transfers between devices: 69.4 us -> none  [column_sums(): return lax.psum_scatter(partial_sum, 'col', scatter_dimension=1, tiled=True)]
    ppermute x0 -> x26, starting transfers between devices: none -> 50.2 us  [the longest x4 23.9 us: sum_row(): lax.ppermute(value, 'row', [(r, r ^ reach) for r in range(ranks)])]
    psum x1 -> x0, waiting for transfers between devices: 33.3 us -> none  [block_totals(): return lax.psum(stacked, 'row')]
  transfers between devices with their start and end apart: 6 -> 28, of which waited for: 4 -> 14; matrix products, arithmetic and copies ran while one was open for 5% -> 14% of each run, Pallas kernels for 0% -> 20%
where the time goes in v1:
time: 335 us; the launch traced here: 336 us
  waiting for transfers between devices  104 us (31%)
  Pallas kernels  101 us (30%)
  starting transfers between devices  50.5 us (15%)
  local copies, waits for them, and re-layouts  30.1 us (9%)
  other arithmetic  29.8 us (9%)
  between operations  14.7 us (4%)
  loops' own time  5.82 us (2%)
    pallas_call x9, Pallas kernels, call(): pl.pallas_call(body, out_shape=outs, in_specs=[SMEM_SPEC] * len(smem) + [...  84.8 us
    ppermute x18, waiting for transfers between devices, swap_col(): return lax.ppermute(value, 'col', [(c, c ^ hop) for c in range(ranks)])  67.3 us
    ppermute x4, waiting for transfers between devices, sum_row(): lax.ppermute(value, 'row', [(r, r ^ reach) for r in range(ranks)])  24.7 us
    ppermute x4, starting transfers between devices, sum_row(): lax.ppermute(value, 'row', [(r, r ^ reach) for r in range(ranks)])  23.9 us
    ppermute x18, starting transfers between devices, swap_col(): return lax.ppermute(value, 'col', [(c, c ^ hop) for c in range(ranks)])  17 us
    pallas_call x1, Pallas kernels, split_root(): pl.pallas_call(split_body, out_shape=jax.ShapeDtypeStruct((rows, 2 * cols...  14.3 us
    ppermute x4, waiting for transfers between devices, turn(): lax.ppermute(piece, ('row', 'col'), [(r * ranks + c, (c ^ u) * ranks + r)...  11.8 us
    ppermute x4, starting transfers between devices, turn(): lax.ppermute(piece, ('row', 'col'), [(r * ranks + c, (c ^ u) * ranks + r)...  9.2 us
  transfers between devices with their start and end apart: 28, of which 14 were waited for; matrix products, arithmetic and copies ran while one was open for 14% of the time, Pallas kernels for 20%

profile of v1, /device:TPU:0, one launch (start us, length us, event | category | flops | bytes accessed | tf_op | source)
XLA Modules:
  0.0 335.6 jit_solution(17674331761988657240)
XLA Ops:
  7.2 1.4 copy.434.one
  8.6 1.4 copy.435.two
  9.9 1.8 shard_map.134
  12.4 316.4 %conditional.1 = (f32[2048,128]{1,0:T(8,128)}, f32[128,128]{1,0:T(8,128)}, f32[2048,256]{1,0:T(8,128)}, f32[128,256]{1,0:T(8,128)}, f32[128,256]{1,0:T(8,128)}) conditional(s32[]{:T(128)} %bitcast.132, (s32[64,4]{0,1:T(4,128)}, s32[64,8]{0,1:T(8,128)}, s32[8]{0:T(128)}, f32[2048,2048]{1,0:T(8,128)}, f32[2048,128]{1,0:T(8,128)}, ...), branch_computations={%region_0.27_spmd, %region_27.54_spmd, %region_54.81_spmd} | conditional | flops 5897845 | bytes 212866816 | solution.py:687
  12.5 1.5 copy.438.pattern
  14.6 2.5 branch_1_fun.11.refs_3_
  18.2 3.0 branch_1_fun.12.refs_0_.refs_4_.packed
  21.6 2.5 collective-permute-start.27
  28.3 0.9 fusion.29
  29.2 1.2 multiply_reduce_fusion.9
  32.9 18.2 %collective-permute-done.27.refs_2_.refs_6_ = f32[2304,128]{1,0:T(8,128)S(1)} collective-permute-done((f32[2304,128]{1,0:T(8,128)}, f32[2304,128]{1,0:T(8,128)S(1)}, u32[]{:S(2)}, u32[]{:S(2)}) %collective-permute-start.27) | collective-permute-done | bytes 1179680 | tf_op jit(solution)/shard_map/cond/branch_1_fun/ppermute | solution.py:409
  51.1 1.6 fusion.31
  52.7 1.4 copy.393
  54.0 2.0 fusion.24
  56.0 1.3 iota_minimum_fusion.5
  57.3 1.4 multiply_reduce_fusion.13
  60.0 2.3 fusion.27
  62.8 2.1 fusion.43
  67.9 14.3 %branch_1_fun.10.root_ref = bf16[2048,4096]{1,0:T(8,128)(2,1)} custom-call(f32[2048,2048]{1,0:T(8,128)} %get-tuple-element.92.source), custom_call_target="tpu_custom_call" | custom-call | tf_op jit(solution)/shard_map/cond/branch_1_fun/pallas_call | solution.py:118
  82.2 1.3 copy.394
  84.9 1.3 copy.397
  86.3 1.4 copy.398
  87.6 1.4 copy.399
  91.1 1.9 add_bitcast_fusion.1.kids
  93.1 1.1 pad_maximum_fusion.7
  94.3 0.9 pad_maximum_fusion.8.link
  95.2 1.0 copy-done.6
  96.5 3.6 %branch_1_fun.13 = (f32[496,128]{1,0:T(8,128)}, f32[496,128]{1,0:T(8,128)}, f32[496,128]{1,0:T(8,128)}, f32[496,128]{1,0:T(8,128)}) custom-call(s32[2]{0:T(128)} %pad_add_fusion.1.where_ref, s32[5]{0:T(128)} %get-tuple-element.485.bases, f32[2304,128]{1,0:T(8,128)} %branch_1_fun.12.refs_0_.refs_4_.packed, f32[2304,128]{1,0:T(8,128)} %copy-done.4, ...), custom_call_target="tpu_custom_call" | custom-call | tf_op jit(solution)/shard_map/cond/branch_1_fun/pallas_call | solution.py:28
  100.1 1.6 collective-permute-start.32
  101.7 2.4 collective-permute-start.33
  104.2 3.6 %collective-permute-start.34 = (f32[496,128]{1,0:T(8,128)}, f32[496,128]{1,0:T(8,128)S(1)}, u32[]{:S(2)}, u32[]{:S(2)}) collective-permute-start(f32[496,128]{1,0:T(8,128)} %get-tuple-element.100), channel_id=1, source_target_pairs={{0,8},{1,12},{2,0},{3,4},{4,9},{5,13},{6,1},{7,5},{8,10},{9,14},{1... | collective-permute-start | bytes 761864 | tf_op jit(solution)/shard_map/cond/branch_1_fun/ppermute | solution.py:427
  107.8 1.6 collective-permute-start.35
  109.4 1.1 collective-permute-done.33
  110.5 10.3 %collective-permute-done.34 = f32[496,128]{1,0:T(8,128)S(1)} collective-permute-done((f32[496,128]{1,0:T(8,128)}, f32[496,128]{1,0:T(8,128)S(1)}, u32[]{:S(2)}, u32[]{:S(2)}) %collective-permute-start.34) | collective-permute-done | bytes 253984 | tf_op jit(solution)/shard_map/cond/branch_1_fun/ppermute | solution.py:427
  121.3 1.0 copy-done.11
  122.4 2.1 constant_dynamic-slice_fusion.15
  124.4 4.4 %collective-permute-start.38 = (f32[1536,128]{1,0:T(8,128)S(1)}, f32[1536,128]{1,0:T(8,128)S(1)}, u32[]{:S(2)}, u32[]{:S(2)}) collective-permute-start(f32[1536,128]{1,0:T(8,128)S(1)} %get-tuple-element.463), channel_id=1, source_target_pairs={{0,3},{1,2},{2,1},{3,0},{4,7},{5,6},{6,5},{7,4},{8,11},{9,10},{10,... | collective-permute-start | bytes 2359304 | tf_op jit(solution)/shard_map/cond/branch_1_fun/ppermute | solution.py:409
  128.8 6.0 %collective-permute-start.37 = (f32[1536,128]{1,0:T(8,128)S(1)}, f32[1536,128]{1,0:T(8,128)S(1)}, u32[]{:S(2)}, u32[]{:S(2)}) collective-permute-start(f32[1536,128]{1,0:T(8,128)S(1)} %get-tuple-element.464), channel_id=1, source_target_pairs={{0,2},{1,3},{2,0},{3,1},{4,6},{5,7},{6,4},{7,5},{8,10},{9,11},{10,... | collective-permute-start | bytes 2359304 | tf_op jit(solution)/shard_map/cond/branch_1_fun/ppermute | solution.py:409
  134.8 6.5 %collective-permute-done.38 = f32[1536,128]{1,0:T(8,128)S(1)} collective-permute-done((f32[1536,128]{1,0:T(8,128)S(1)}, f32[1536,128]{1,0:T(8,128)S(1)}, u32[]{:S(2)}, u32[]{:S(2)}) %collective-permute-start.38) | collective-permute-done | bytes 786464 | tf_op jit(solution)/shard_map/cond/branch_1_fun/ppermute | solution.py:409
  141.3 22.4 %collective-permute-done.37 = f32[1536,128]{1,0:T(8,128)S(1)} collective-permute-done((f32[1536,128]{1,0:T(8,128)S(1)}, f32[1536,128]{1,0:T(8,128)S(1)}, u32[]{:S(2)}, u32[]{:S(2)}) %collective-permute-start.37) | collective-permute-done | bytes 786464 | tf_op jit(solution)/shard_map/cond/branch_1_fun/ppermute | solution.py:409
  163.8 1.9 pad_maximum_fusion.5.gathered
  165.6 22.7 %branch_1_fun.14 = (f32[1536,128]{1,0:T(8,128)}, f32[1536,128]{1,0:T(8,128)}, f32[1536,128]{1,0:T(8,128)}, f32[1536,128]{1,0:T(8,128)}, f32[6144,128]{1,0:T(8,128)}) custom-call(s32[2]{0:T(128)} %pad_add_fusion.1.where_ref, s32[328]{0:T(512)} %reshape.752.table, bf16[2048,4096]{1,0:T(8,128)(2,1)} %branch_1_fun.10.root_ref, ...), custom_call_target="tpu_custom_call" | custom-call | tf_op jit(solution)/shard_map/cond/branch_1_fun/pallas_call | solution.py:28
  188.4 2.5 collective-permute-done.40
  190.9 1.2 add.469
  192.1 1.5 collective-permute-start.41
  194.3 10.1 %branch_1_fun.15.refs_0_ = f32[9216,128]{1,0:T(8,128)} custom-call(s32[656]{0:T(1024)} %reshape.753.table, f32[6144,128]{1,0:T(8,128)} %get-tuple-element.108.firsts, f32[128,1024]{1,0:T(8,128)} %pad_maximum_fusion.8.link), custom_call_target="tpu_custom_call" | custom-call | tf_op jit(solution)/shard_map/cond/branch_1_fun/pallas_call | solution.py:28
  204.4 7.3 %collective-permute-done.41.refs_2_ = f32[1536,128]{1,0:T(8,128)S(1)} collective-permute-done((f32[1536,128]{1,0:T(8,128)S(1)}, f32[1536,128]{1,0:T(8,128)S(1)}, u32[]{:S(2)}, u32[]{:S(2)}) %collective-permute-start.41) | collective-permute-done | bytes 786464 | tf_op jit(solution)/shard_map/cond/branch_1_fun/ppermute | solution.py:409
  212.9 10.2 %branch_1_fun.16 = (f32[2048,128]{1,0:T(8,128)}, f32[384,128]{1,0:T(8,128)}, f32[1536,128]{1,0:T(8,128)}) custom-call(s32[2]{0:T(128)} %pad_add_fusion.1.where_ref, s32[64,4]{1,0:T(8,128)} %copy.438.pattern, s32[64,4]{1,0:T(8,128)} %bitcast.175, s32[64,8]{1,0:T(8,128)} %copy.439.pattern.pattern_two, s32[64,8]{1,0:T(8,128)} %copy.401.position_two.position, ...), custom_call_target="tpu_custom_call" | custom-call | tf_op jit(solution)/shard_map/cond/branch_1_fun/pallas_call | solution.py:28
  223.1 23.1 %branch_1_fun.17 = (f32[2304,128]{1,0:T(8,128)}, f32[2304,128]{1,0:T(8,128)}, f32[2304,128]{1,0:T(8,128)}, f32[2304,128]{1,0:T(8,128)}) custom-call(s32[2]{0:T(128)} %pad_add_fusion.1.where_ref, s32[656]{0:T(1024)} %reshape.753.table, bf16[2048,4096]{1,0:T(8,128)(2,1)} %branch_1_fun.10.root_ref, f32[7936,128]{1,0:T(8,128)} %all-gather.13.cloned.1.call-done.gathered, ...), custom_call_target="tpu_custom_call" | custom-call | tf_op jit(solution)/shard_map/cond/branch_1_fun/pallas_call | solution.py:28
  246.9 2.5 collective-permute-done.42
  249.4 1.4 add.470
  250.9 5.2 %collective-permute-start.43 = (f32[384,128]{1,0:T(8,128)S(1)}, f32[384,128]{1,0:T(8,128)S(1)}, u32[]{:S(2)}, u32[]{:S(2)}) collective-permute-start(f32[384,128]{1,0:T(8,128)S(1)} %copy-done.42), channel_id=1, source_target_pairs={{0,4},{4,0},{8,12},{12,8},{1,5},{5,1},{9,13},{13,9},{2,6},{6,2},{1... | collective-permute-start | bytes 589832 | tf_op jit(solution)/shard_map/cond/branch_1_fun/ppermute | solution.py:447
  256.1 4.9 %collective-permute-done.43 = f32[384,128]{1,0:T(8,128)S(1)} collective-permute-done((f32[384,128]{1,0:T(8,128)S(1)}, f32[384,128]{1,0:T(8,128)S(1)}, u32[]{:S(2)}, u32[]{:S(2)}) %collective-permute-start.43) | collective-permute-done | bytes 196640 | tf_op jit(solution)/shard_map/cond/branch_1_fun/ppermute | solution.py:447
  261.0 12.1 %collective-permute-start.44 = (f32[384,128]{1,0:T(8,128)S(1)}, f32[384,128]{1,0:T(8,128)S(1)}, u32[]{:S(2)}, u32[]{:S(2)}) collective-permute-start(f32[384,128]{1,0:T(8,128)S(1)} %add.471), channel_id=1, source_target_pairs={{0,8},{4,12},{8,0},{12,4},{1,9},{5,13},{9,1},{13,5},{2,10},{6,14},... | collective-permute-start | bytes 589832 | tf_op jit(solution)/shard_map/cond/branch_1_fun/ppermute | solution.py:447
  273.1 8.3 %collective-permute-done.44 = f32[384,128]{1,0:T(8,128)S(1)} collective-permute-done((f32[384,128]{1,0:T(8,128)S(1)}, f32[384,128]{1,0:T(8,128)S(1)}, u32[]{:S(2)}, u32[]{:S(2)}) %collective-permute-start.44) | collective-permute-done | bytes 196640 | tf_op jit(solution)/shard_map/cond/branch_1_fun/ppermute | solution.py:447
  282.1 2.6 branch_1_fun.18
  285.4 7.8 %collective-permute-done.48 = f32[256,256]{1,0:T(8,128)} collective-permute-done((f32[256,256]{1,0:T(8,128)}, f32[256,256]{1,0:T(8,128)}, u32[]{:S(2)}, u32[]{:S(2)}) %collective-permute-start.48) | collective-permute-done | bytes 262176 | tf_op jit(solution)/shard_map/cond/branch_1_fun/ppermute | solution.py:409
  298.5 1.3 pad_maximum_fusion.6
  299.8 1.0 copy-done.13
  301.2 7.0 %branch_1_fun.19 = (f32[2048,256]{1,0:T(8,128)}, f32[128,256]{1,0:T(8,128)}, f32[2304,128]{1,0:T(8,128)}) custom-call(s32[2]{0:T(128)} %pad_add_fusion.1.where_ref, s32[64,8]{1,0:T(8,128)} %copy.439.pattern.pattern_two, s32[64,8]{1,0:T(8,128)} %copy.401.position_two.position, f32[2304,128]{1,0:T(8,128)} %get-tuple-element.118.mine, f32[2304,128]{1,0:T(8,128)} %copy-done.13, ...), custom_call_target="tpu_custom_call" | custom-call | tf_op jit(solution)/shard_map/cond/branch_1_fun/pallas_call | solution.py:28
  308.2 6.1 %collective-permute-done.50 = f32[128,256]{1,0:T(8,128)S(1)} collective-permute-done((f32[128,256]{1,0:T(8,128)}, f32[128,256]{1,0:T(8,128)S(1)}, u32[]{:S(2)}, u32[]{:S(2)}) %collective-permute-start.50) | collective-permute-done | bytes 131104 | tf_op jit(solution)/shard_map/cond/branch_1_fun/ppermute | solution.py:447
  314.3 0.9 add.481
  315.3 6.7 %collective-permute-start.51 = (f32[128,256]{1,0:T(8,128)S(1)}, f32[128,256]{1,0:T(8,128)S(1)}, u32[]{:S(2)}, u32[]{:S(2)}) collective-permute-start(f32[128,256]{1,0:T(8,128)S(1)} %add.481), channel_id=1, source_target_pairs={{0,8},{4,12},{8,0},{12,4},{1,9},{5,13},{9,1},{13,5},{2,10},{6,14},... | collective-permute-start | bytes 393224 | tf_op jit(solution)/shard_map/cond/branch_1_fun/ppermute | solution.py:447
  322.6 5.4 %collective-permute-done.51 = f32[128,256]{1,0:T(8,128)S(1)} collective-permute-done((f32[128,256]{1,0:T(8,128)S(1)}, f32[128,256]{1,0:T(8,128)S(1)}, u32[]{:S(2)}, u32[]{:S(2)}) %collective-permute-start.51) | collective-permute-done | bytes 131104 | tf_op jit(solution)/shard_map/cond/branch_1_fun/ppermute | solution.py:447
  (145 shorter events, 24.1 us)
Async XLA Ops:
  12.4 5.1 %copy-start.39 = (s32[64,8]{0,1:T(8,128)S(1)}, s32[64,8]{0,1:T(8,128)}, u32[]{:S(2)}) copy-start(s32[64,8]{0,1:T(8,128)} %get-tuple-element.338) | copy-start | bytes 6148 | tf_op jit(solution)/shard_map/cond
  12.4 5.8 %copy-start.1 = (f32[2048,256]{1,0:T(8,128)S(1)}, f32[2048,256]{1,0:T(8,128)}, u32[]{:S(2)}) copy-start(f32[2048,256]{1,0:T(8,128)} %get-tuple-element.95.source) | copy-start | bytes 6291460 | tf_op jit(solution)/shard_map/cond
  12.4 109.9 %all-gather.11.cloned.1.call-start = ((), (), s32[]{:S(2)}) async-start(), calls=%async_computation.2 | async-start | bytes 3932160 | tf_op jit(solution)/shard_map/cond/branch_1_fun/all_gather | solution.py:509
  14.6 9.8 %copy-start.27 = (s32[64,4]{1,0:T(8,128)S(1)}, s32[64,4]{1,0:T(8,128)}, u32[]{:S(2)}) copy-start(s32[64,4]{1,0:T(8,128)} %copy.438.pattern) | copy-start | bytes 3076 | tf_op jit(solution)/shard_map/cond
  17.1 13.9 %copy-start.45 = (s32[8]{0:T(128)S(1)}, s32[8]{0:T(128)}, u32[]{:S(2)}) copy-start(s32[8]{0:T(128)} %get-tuple-element.91) | copy-start | bytes 100 | tf_op jit(solution)/shard_map/cond
  17.2 206.0 %all-gather.13.cloned.1.call-start = ((), (), s32[]{:S(2)}) async-start(), calls=%async_computation.3 | async-start | bytes 5079040 | tf_op jit(solution)/shard_map/cond/branch_1_fun/all_gather | solution.py:566
  18.1 8.7 %copy-start.25 = (s32[64,8]{1,0:T(8,128)S(1)}, s32[64,8]{1,0:T(8,128)}, u32[]{:S(2)}) copy-start(s32[64,8]{1,0:T(8,128)} %copy.439.pattern.pattern_two) | copy-start | bytes 6148 | tf_op jit(solution)/shard_map/cond
  21.1 74.0 %collective-permute-start.26 = (f32[2304,128]{1,0:T(8,128)}, f32[2304,128]{1,0:T(8,128)S(1)}, u32[]{:S(2)}, u32[]{:S(2)}) collective-permute-start(f32[2304,128]{1,0:T(8,128)} %branch_1_fun.12.refs_0_.refs_4_.packed), channel_id=1, source_target_pairs={{0,1},{1,0},{2,3},{3,2},{4,5},{5,4},{6,7},{7,6},{8,9},{9,8},{10,11... | collective-permute-start | bytes 3538952 | tf_op jit(solution)/shard_map/cond/branch_1_fun/ppermute | solution.py:409
  21.6 29.5 %collective-permute-start.27 = (f32[2304,128]{1,0:T(8,128)}, f32[2304,128]{1,0:T(8,128)S(1)}, u32[]{:S(2)}, u32[]{:S(2)}) collective-permute-start(f32[2304,128]{1,0:T(8,128)} %branch_1_fun.12.refs_0_.refs_4_.packed), channel_id=1, source_target_pairs={{0,2},{1,3},{2,0},{3,1},{4,6},{5,7},{6,4},{7,5},{8,10},{9,11},{10,... | collective-permute-start | bytes 3538952 | tf_op jit(solution)/shard_map/cond/branch_1_fun/ppermute | solution.py:409
  24.0 38.3 %collective-permute-start.30 = (f32[128,256]{1,0:T(8,128)}, f32[128,256]{1,0:T(8,128)}, u32[]{:S(2)}, u32[]{:S(2)}) collective-permute-start(f32[128,256]{1,0:T(8,128)} %get-tuple-element.96), channel_id=1, source_target_pairs={{0,2},{1,3},{2,0},{3,1},{4,6},{5,7},{6,4},{7,5},{8,10},{9,11},{10,... | collective-permute-start | bytes 393224 | tf_op jit(solution)/shard_map/cond/branch_1_fun/ppermute | solution.py:409
  24.1 69.0 %collective-permute-start.29 = (f32[128,256]{1,0:T(8,128)}, f32[128,256]{1,0:T(8,128)}, u32[]{:S(2)}, u32[]{:S(2)}) collective-permute-start(f32[128,256]{1,0:T(8,128)} %get-tuple-element.96), channel_id=1, source_target_pairs={{0,1},{1,0},{2,3},{3,2},{4,5},{5,4},{6,7},{7,6},{8,9},{9,8},{10,11... | collective-permute-start | bytes 393224 | tf_op jit(solution)/shard_map/cond/branch_1_fun/ppermute | solution.py:409
  25.6 7.3 %copy-start.36 = (s32[4,16,4,1]{2,1,0,3:T(8,128)}, s32[4,16,4,1]{2,1,0,3:T(8,128)S(1)}, u32[]{:S(2)}) copy-start(s32[4,16,4,1]{2,1,0,3:T(8,128)S(1)} %copy.377) | copy-start | bytes 3076 | tf_op jit(solution)/shard_map/cond
  25.9 6.9 %copy-start.48 = (s32[16,4]{0,1:T(4,128)}, s32[16,4]{0,1:T(4,128)S(1)}, u32[]{:S(2)}) copy-start(s32[16,4]{0,1:T(4,128)S(1)} %copy.383) | copy-start | bytes 772 | tf_op jit(solution)/shard_map/cond
  26.0 6.9 %copy-start.53 = (s32[4]{0:T(128)}, s32[4]{0:T(128)S(1)}, u32[]{:S(2)}) copy-start(s32[4]{0:T(128)S(1)} %get-tuple-element.418) | copy-start | bytes 52 | tf_op jit(solution)/shard_map/cond
  26.0 6.9 %copy-start.54 = (s32[4]{0:T(128)}, s32[4]{0:T(128)S(1)}, u32[]{:S(2)}) copy-start(s32[4]{0:T(128)S(1)} %get-tuple-element.480) | copy-start | bytes 52 | tf_op jit(solution)/shard_map/cond
  26.1 6.8 %copy-start.49 = (s32[16,4]{0,1:T(4,128)}, s32[16,4]{0,1:T(4,128)S(1)}, u32[]{:S(2)}) copy-start(s32[16,4]{0,1:T(4,128)S(1)} %copy.384) | copy-start | bytes 772 | tf_op jit(solution)/shard_map/cond
  26.9 6.0 %copy-start.50 = (s32[8]{0:T(128)}, s32[8]{0:T(128)S(1)}, u32[]{:S(2)}) copy-start(s32[8]{0:T(128)S(1)} %get-tuple-element.414) | copy-start | bytes 100 | tf_op jit(solution)/shard_map/cond
  26.9 6.0 %copy-start.52 = (s32[8]{0:T(128)}, s32[8]{0:T(128)S(1)}, u32[]{:S(2)}) copy-start(s32[8]{0:T(128)S(1)} %get-tuple-element.476) | copy-start | bytes 100 | tf_op jit(solution)/shard_map/cond
  51.1 31.1 %copy-start.5 = (f32[2304,128]{1,0:T(8,128)}, f32[2304,128]{1,0:T(8,128)S(1)}, u32[]{:S(2)}) copy-start(f32[2304,128]{1,0:T(8,128)S(1)} %collective-permute-done.27.refs_2_.refs_6_) | copy-start | bytes 3538948 | tf_op jit(solution)/shard_map/cond
  51.1 44.1 %collective-permute-start.28 = (f32[2304,128]{1,0:T(8,128)S(1)}, f32[2304,128]{1,0:T(8,128)S(1)}, u32[]{:S(2)}, u32[]{:S(2)}) collective-permute-start(f32[2304,128]{1,0:T(8,128)S(1)} %collective-permute-done.27.refs_2_.refs_6_), channel_id=1, source_target_pairs={{0,1},{1,0},{2,3},{3,2},{4,5},{5,4},{6,7},{7,6},{8,9},{9,8},{10,11... | collective-permute-start | bytes 3538952 | tf_op jit(solution)/shard_map/cond/branch_1_fun/ppermute | solution.py:409
  62.3 30.8 %collective-permute-start.31 = (f32[128,256]{1,0:T(8,128)}, f32[128,256]{1,0:T(8,128)}, u32[]{:S(2)}, u32[]{:S(2)}) collective-permute-start(f32[128,256]{1,0:T(8,128)} %collective-permute-done.30), channel_id=1, source_target_pairs={{0,1},{1,0},{2,3},{3,2},{4,5},{5,4},{6,7},{7,6},{8,9},{9,8},{10,11... | collective-permute-start | bytes 393224 | tf_op jit(solution)/shard_map/cond/branch_1_fun/ppermute | solution.py:409
  67.9 15.6 %copy-start.51 = (s32[8]{0:T(128)S(1)}, s32[8]{0:T(128)}, u32[]{:S(2)}) copy-start(s32[8]{0:T(128)} %copy-done.50) | copy-start | bytes 100 | tf_op jit(solution)/shard_map/cond
  67.9 21.1 %copy-start.47 = (s32[16,8]{1,0:T(8,128)S(1)}, s32[16,8]{1,0:T(8,128)}, u32[]{:S(2)}) copy-start(s32[16,8]{1,0:T(8,128)} %get-tuple-element.372) | copy-start | bytes 1540 | tf_op jit(solution)/shard_map/cond
  95.1 1.0 copy-start.6
  95.1 1.4 copy-start.4
  100.1 9.2 %collective-permute-start.32 = (f32[496,128]{1,0:T(8,128)}, f32[496,128]{1,0:T(8,128)S(1)}, u32[]{:S(2)}, u32[]{:S(2)}) collective-permute-start(f32[496,128]{1,0:T(8,128)} %get-tuple-element.98), channel_id=1, source_target_pairs={{0,0},{1,4},{2,8},{3,12},{4,1},{5,5},{6,9},{7,13},{8,2},{9,6},{10,... | collective-permute-start | bytes 761864 | tf_op jit(solution)/shard_map/cond/branch_1_fun/ppermute | solution.py:427
  101.7 8.7 %collective-permute-start.33 = (f32[496,128]{1,0:T(8,128)}, f32[496,128]{1,0:T(8,128)S(1)}, u32[]{:S(2)}, u32[]{:S(2)}) collective-permute-start(f32[496,128]{1,0:T(8,128)} %get-tuple-element.99), channel_id=1, source_target_pairs={{0,4},{1,0},{2,12},{3,8},{4,5},{5,1},{6,13},{7,9},{8,6},{9,2},{10,... | collective-permute-start | bytes 761864 | tf_op jit(solution)/shard_map/cond/branch_1_fun/ppermute | solution.py:427
  104.2 16.6 %collective-permute-start.34 = (f32[496,128]{1,0:T(8,128)}, f32[496,128]{1,0:T(8,128)S(1)}, u32[]{:S(2)}, u32[]{:S(2)}) collective-permute-start(f32[496,128]{1,0:T(8,128)} %get-tuple-element.100), channel_id=1, source_target_pairs={{0,8},{1,12},{2,0},{3,4},{4,9},{5,13},{6,1},{7,5},{8,10},{9,14},{1... | collective-permute-start | bytes 761864 | tf_op jit(solution)/shard_map/cond/branch_1_fun/ppermute | solution.py:427
  107.8 13.5 %collective-permute-start.35 = (f32[496,128]{1,0:T(8,128)}, f32[496,128]{1,0:T(8,128)S(1)}, u32[]{:S(2)}, u32[]{:S(2)}) collective-permute-start(f32[496,128]{1,0:T(8,128)} %get-tuple-element.101), channel_id=1, source_target_pairs={{0,12},{1,8},{2,4},{3,0},{4,13},{5,9},{6,5},{7,1},{8,14},{9,10},{1... | collective-permute-start | bytes 761864 | tf_op jit(solution)/shard_map/cond/branch_1_fun/ppermute | solution.py:427
  121.3 1.0 copy-start.11
  124.4 16.9 %collective-permute-start.38 = (f32[1536,128]{1,0:T(8,128)S(1)}, f32[1536,128]{1,0:T(8,128)S(1)}, u32[]{:S(2)}, u32[]{:S(2)}) collective-permute-start(f32[1536,128]{1,0:T(8,128)S(1)} %get-tuple-element.463), channel_id=1, source_target_pairs={{0,3},{1,2},{2,1},{3,0},{4,7},{5,6},{6,5},{7,4},{8,11},{9,10},{10,... | collective-permute-start | bytes 2359304 | tf_op jit(solution)/shard_map/cond/branch_1_fun/ppermute | solution.py:409
  128.8 35.0 %collective-permute-start.37 = (f32[1536,128]{1,0:T(8,128)S(1)}, f32[1536,128]{1,0:T(8,128)S(1)}, u32[]{:S(2)}, u32[]{:S(2)}) collective-permute-start(f32[1536,128]{1,0:T(8,128)S(1)} %get-tuple-element.464), channel_id=1, source_target_pairs={{0,2},{1,3},{2,0},{3,1},{4,6},{5,7},{6,4},{7,5},{8,10},{9,11},{10,... | collective-permute-start | bytes 2359304 | tf_op jit(solution)/shard_map/cond/branch_1_fun/ppermute | solution.py:409
  134.8 28.9 %collective-permute-start.36 = (f32[1536,128]{1,0:T(8,128)S(1)}, f32[1536,128]{1,0:T(8,128)S(1)}, u32[]{:S(2)}, u32[]{:S(2)}) collective-permute-start(f32[1536,128]{1,0:T(8,128)S(1)} %get-tuple-element.465), channel_id=1, source_target_pairs={{0,1},{1,0},{2,3},{3,2},{4,5},{5,4},{6,7},{7,6},{8,9},{9,8},{10,11... | collective-permute-start | bytes 2359304 | tf_op jit(solution)/shard_map/cond/branch_1_fun/ppermute | solution.py:409
  188.3 2.6 collective-permute-start.40
  192.1 19.6 %collective-permute-start.41 = (f32[1536,128]{1,0:T(8,128)S(1)}, f32[1536,128]{1,0:T(8,128)S(1)}, u32[]{:S(2)}, u32[]{:S(2)}) collective-permute-start(f32[1536,128]{1,0:T(8,128)S(1)} %add.469), channel_id=1, source_target_pairs={{0,2},{1,3},{2,0},{3,1},{4,6},{5,7},{6,4},{7,5},{8,10},{9,11},{10,... | collective-permute-start | bytes 2359304 | tf_op jit(solution)/shard_map/cond/branch_1_fun/ppermute | solution.py:409
  193.6 18.1 %collective-permute-start.39 = (f32[1536,128]{1,0:T(8,128)}, f32[1536,128]{1,0:T(8,128)S(1)}, u32[]{:S(2)}, u32[]{:S(2)}) collective-permute-start(f32[1536,128]{1,0:T(8,128)} %get-tuple-element.104), channel_id=1, source_target_pairs={{0,1},{1,0},{2,3},{3,2},{4,5},{5,4},{6,7},{7,6},{8,9},{9,8},{10,11... | collective-permute-start | bytes 2359304 | tf_op jit(solution)/shard_map/cond/branch_1_fun/ppermute | solution.py:409
  211.7 0.9 copy-start.22
  211.7 1.2 copy-start.23
  246.3 4.6 %copy-start.42 = (f32[384,128]{1,0:T(8,128)S(1)}, f32[384,128]{1,0:T(8,128)}, u32[]{:S(2)}) copy-start(f32[384,128]{1,0:T(8,128)} %get-tuple-element.116) | copy-start | bytes 589828 | tf_op jit(solution)/shard_map/cond
  246.3 35.8 %copy-start.33 = (f32[128,128]{1,0:T(8,128)S(1)}, f32[128,128]{1,0:T(8,128)}, u32[]{:S(2)}) copy-start(f32[128,128]{1,0:T(8,128)} %get-tuple-element.111.diag) | copy-start | bytes 196612 | tf_op jit(solution)/shard_map/cond
  246.3 3.1 collective-permute-start.42
  246.4 53.4 %collective-permute-start.45 = (f32[2304,128]{1,0:T(8,128)}, f32[2304,128]{1,0:T(8,128)S(1)}, u32[]{:S(2)}, u32[]{:S(2)}) collective-permute-start(f32[2304,128]{1,0:T(8,128)} %get-tuple-element.119), channel_id=1, source_target_pairs={{0,1},{1,0},{2,3},{3,2},{4,5},{5,4},{6,7},{7,6},{8,9},{9,8},{10,11... | collective-permute-start | bytes 3538952 | tf_op jit(solution)/shard_map/cond/branch_1_fun/ppermute | solution.py:409
  250.8 49.0 %collective-permute-start.46 = (f32[2304,128]{1,0:T(8,128)S(1)}, f32[2304,128]{1,0:T(8,128)S(1)}, u32[]{:S(2)}, u32[]{:S(2)}) collective-permute-start(f32[2304,128]{1,0:T(8,128)S(1)} %add.470), channel_id=1, source_target_pairs={{0,2},{1,3},{2,0},{3,1},{4,6},{5,7},{6,4},{7,5},{8,10},{9,11},{10,... | collective-permute-start | bytes 3538952 | tf_op jit(solution)/shard_map/cond/branch_1_fun/ppermute | solution.py:409
  250.9 10.1 %collective-permute-start.43 = (f32[384,128]{1,0:T(8,128)S(1)}, f32[384,128]{1,0:T(8,128)S(1)}, u32[]{:S(2)}, u32[]{:S(2)}) collective-permute-start(f32[384,128]{1,0:T(8,128)S(1)} %copy-done.42), channel_id=1, source_target_pairs={{0,4},{4,0},{8,12},{12,8},{1,5},{5,1},{9,13},{13,9},{2,6},{6,2},{1... | collective-permute-start | bytes 589832 | tf_op jit(solution)/shard_map/cond/branch_1_fun/ppermute | solution.py:447
  261.0 20.3 %collective-permute-start.44 = (f32[384,128]{1,0:T(8,128)S(1)}, f32[384,128]{1,0:T(8,128)S(1)}, u32[]{:S(2)}, u32[]{:S(2)}) collective-permute-start(f32[384,128]{1,0:T(8,128)S(1)} %add.471), channel_id=1, source_target_pairs={{0,8},{4,12},{8,0},{12,4},{1,9},{5,13},{9,1},{13,5},{2,10},{6,14},... | collective-permute-start | bytes 589832 | tf_op jit(solution)/shard_map/cond/branch_1_fun/ppermute | solution.py:447
  284.7 8.5 %collective-permute-start.48 = (f32[256,256]{1,0:T(8,128)}, f32[256,256]{1,0:T(8,128)}, u32[]{:S(2)}, u32[]{:S(2)}) collective-permute-start(f32[256,256]{1,0:T(8,128)} %get-tuple-element.121), channel_id=1, source_target_pairs={{0,2},{1,3},{2,0},{3,1},{4,6},{5,7},{6,4},{7,5},{8,10},{9,11},{10,... | collective-permute-start | bytes 786440 | tf_op jit(solution)/shard_map/cond/branch_1_fun/ppermute | solution.py:409
  285.3 13.1 %collective-permute-start.47 = (f32[256,256]{1,0:T(8,128)}, f32[256,256]{1,0:T(8,128)}, u32[]{:S(2)}, u32[]{:S(2)}) collective-permute-start(f32[256,256]{1,0:T(8,128)} %get-tuple-element.121), channel_id=1, source_target_pairs={{0,1},{1,0},{2,3},{3,2},{4,5},{5,4},{6,7},{7,6},{8,9},{9,8},{10,11... | collective-permute-start | bytes 786440 | tf_op jit(solution)/shard_map/cond/branch_1_fun/ppermute | solution.py:409
  293.2 5.3 %collective-permute-start.49 = (f32[256,256]{1,0:T(8,128)}, f32[256,256]{1,0:T(8,128)}, u32[]{:S(2)}, u32[]{:S(2)}) collective-permute-start(f32[256,256]{1,0:T(8,128)} %collective-permute-done.48), channel_id=1, source_target_pairs={{0,1},{1,0},{2,3},{3,2},{4,5},{5,4},{6,7},{7,6},{8,9},{9,8},{10,11... | collective-permute-start | bytes 786440 | tf_op jit(solution)/shard_map/cond/branch_1_fun/ppermute | solution.py:409
  299.8 1.0 copy-start.13
  299.8 1.4 copy-start.14
  301.2 26.8 %copy-start.16 = (f32[128,256]{1,0:T(8,128)S(1)}, f32[128,256]{1,0:T(8,128)}, u32[]{:S(2)}) copy-start(f32[128,256]{1,0:T(8,128)} %get-tuple-element.122) | copy-start | bytes 393220 | tf_op jit(solution)/shard_map/cond
  308.2 6.1 %collective-permute-start.50 = (f32[128,256]{1,0:T(8,128)}, f32[128,256]{1,0:T(8,128)S(1)}, u32[]{:S(2)}, u32[]{:S(2)}) collective-permute-start(f32[128,256]{1,0:T(8,128)} %get-tuple-element.123), channel_id=1, source_target_pairs={{0,4},{4,0},{8,12},{12,8},{1,5},{5,1},{9,13},{13,9},{2,6},{6,2},{1... | collective-permute-start | bytes 393224 | tf_op jit(solution)/shard_map/cond/branch_1_fun/ppermute | solution.py:447
  315.3 12.8 %collective-permute-start.51 = (f32[128,256]{1,0:T(8,128)S(1)}, f32[128,256]{1,0:T(8,128)S(1)}, u32[]{:S(2)}, u32[]{:S(2)}) collective-permute-start(f32[128,256]{1,0:T(8,128)S(1)} %add.481), channel_id=1, source_target_pairs={{0,8},{4,12},{8,0},{12,4},{1,9},{5,13},{9,1},{13,5},{2,10},{6,14},... | collective-permute-start | bytes 393224 | tf_op jit(solution)/shard_map/cond/branch_1_fun/ppermute | solution.py:447
Sparse Core Ops, SparseCore 0:
  17.3 66.2 all-gather.10
  122.4 87.8 all-gather.12
